TPU v7x, 32 devices: a whole 2x2x4 slice. The times are simulated.
32 devices in a mesh: dp: 2 (over x), context: 16 (over z, y, core).
Axes of the slice: x: 2, y: 2, z: 4, core: 2. Of those that a mesh axis runs over, the one named last changes fastest.
Arguments:
- grad_out: bfloat16 [2, 2048, 4096], P('dp', 'context'), may hold values from -6 to 6
- attn: bfloat16 [2, 2048, 4096], P('dp', 'context'), may hold values from -0.09375 to 0.09375
- w_out: bfloat16 [4096, 4096], P('context'), may hold values from -0.09375 to 0.09375
Outputs:
- grad_attn: bfloat16 [2, 2048, 4096], P('dp', None, 'context')
- grad_w: bfloat16 [4096, 4096], P('context')
All inputs are finite; a program needn't handle non-finite values.
Results may differ from a plain program's by a relative error of at most 0.013.
Values may be sent and summed in bfloat16 or wider, within the bound.
A program may use at most 128 MiB of HBM per device.

v0:
```python
import jax
import jax.numpy as jnp
from jax import lax
from jax.sharding import PartitionSpec as P


def accumulate(heads_view, weight_cols, block_rows):
    local_part = lax.dot_general(
        block_rows, weight_cols, (((1,), (1,)), ((), ())), preferred_element_type=jnp.float32
    )
    weight_acc = lax.dot_general(
        heads_view, block_rows, (((0,), (0,)), ((), ())), preferred_element_type=jnp.float32
    )
    return (local_part, weight_acc)


def local(grad_out, attn, w_out):
    cotangent = grad_out[0]
    activations = attn[0]
    heads_view = lax.all_to_all(activations, "context", split_axis=1, concat_axis=0, tiled=True)
    head_acc, weight_acc = accumulate(
        heads_view, w_out, lax.all_gather(cotangent, "context", axis=0, tiled=True)
    )
    weight_sum = lax.psum(weight_acc.astype(jnp.bfloat16), "dp")
    return (head_acc.astype(jnp.bfloat16)[None], weight_sum)


def solution(mesh):
    in_specs = (P("dp", "context", None), P("dp", "context", None), P("context", None))
    out_specs = (P("dp", None, "context"), P("context", None))
    return jax.shard_map(local, mesh=mesh, in_specs=in_specs, out_specs=out_specs, check_vma=False)
```

profile of v0, /device:TPU:0, one launch (start us, length us, event | category | flops | bytes accessed | tf_op | source)
XLA Modules:
  0.0 239.9 jit_solution(10566941267229091638)
XLA Ops:
  7.2 0.0 copy-start
  7.2 0.0 all-gather.3.cloned.1.call-start
  7.2 0.7 all-gather.3.cloned.1.call-update
  7.9 0.0 all-reduce.2.cloned.1.call-start
  8.0 1.6 copy.5
  9.6 47.5 %all_to_all.19 = bf16[128,16,256]{0,2,1:T(8,128)(2,1)} all-to-all(bf16[128,16,256]{0,2,1:T(8,128)(2,1)S(1)} %bitcast.20), channel_id=1, replica_groups=mesh['dp'=2,'context'=16] {'context'}, dimensions={1} | all-to-all | bytes 2097152 | tf_op jit(solution)/shard_map/all_to_all | solution.py:20
  57.1 1.5 copy.6
  58.6 98.5 %all-gather.3.cloned.1.call-done = bf16[1,2048,4096]{2,1,0:T(8,128)(2,1)} async-done(((bf16[1,128,4096]{2,1,0:T(8,128)(2,1)}), bf16[1,2048,4096]{2,1,0:T(8,128)(2,1)}) %all-gather.3.cloned.1.call-update) | async-done | bytes 16777232 | tf_op jit(solution)/shard_map/all_gather | solution.py:22
  157.1 11.5 %fusion.4 = bf16[256,4096]{1,0:T(8,128)(2,1)} fusion(bf16[2048,256]{1,0:T(8,128)(2,1)S(1)} %bitcast.18, bf16[1,2048,4096]{2,1,0:T(8,128)(2,1)} %all-gather.3.cloned.1.call-done), kind=kOutput, calls=%fused_computation.4 | convolution fusion | flops 4296015872 | bytes 19922944 | tf_op jit(solution)/shard_map/dot_general | solution.py:11
  168.6 0.0 all-reduce.2.cloned.1.call-update
  168.6 0.0 copy-done
  168.7 9.9 %fusion.10 = bf16[1,2048,256]{2,1,0:T(8,128)(2,1)} fusion(bf16[256,4096]{1,0:T(8,128)(2,1)S(1)} %copy-done, bf16[1,2048,4096]{2,1,0:T(8,128)(2,1)} %all-gather.3.cloned.1.call-done), kind=kOutput, calls=%fused_computation.6 | convolution fusion | flops 4295491584 | bytes 19922944 | tf_op jit(solution)/shard_map/dot_general | solution.py:8
  178.6 51.4 %all-reduce.2.cloned.1.call-done = bf16[256,4096]{1,0:T(8,128)(2,1)} async-done(((bf16[256,4096]{1,0:T(8,128)(2,1)}), bf16[256,4096]{1,0:T(8,128)(2,1)}) %all-reduce.2.cloned.1.call-update) | async-done | bytes 2097168 | tf_op jit(solution)/shard_map/psum | solution.py:24
  230.0 3.1 %copy.8 = bf16[256,4096]{1,0:T(8,128)(2,1)} copy(bf16[256,4096]{1,0:T(8,128)(2,1)} %all-reduce.2.cloned.1.call-done) | data formatting | bytes 4194304
Async XLA Ops:
  7.2 161.5 %copy-start = (bf16[256,4096]{1,0:T(8,128)(2,1)S(1)}, bf16[256,4096]{1,0:T(8,128)(2,1)}, u32[]{:S(2)}) copy-start(bf16[256,4096]{1,0:T(8,128)(2,1)} %param.5) | copy-start | bytes 6291460
  7.2 150.0 %all-gather.3.cloned.1.call-start = ((), (), s32[]{:S(2)}) async-start(), calls=%async_computation.2 | async-start | bytes 17825792 | tf_op jit(solution)/shard_map/all_gather | solution.py:22
  7.9 222.0 %all-reduce.2.cloned.1.call-start = ((), (), s32[]{:S(2)}) async-start(), calls=%async_computation.1 | async-start | bytes 4194304 | tf_op jit(solution)/shard_map/psum | solution.py:24
Sparse Core Ops, SparseCore 0:
  10.1 146.9 all-gather.2
  168.8 61.1 all-reduce.1
where the time goes:
time: 240 us
  waiting for transfers between devices  151 us (63%)
  blocking collectives  47.5 us (20%)
  matrix products  21.4 us (9%)
  between operations  14.1 us (6%)
  local copies, waits for them, and re-layouts  6.24 us (3%)
    all_gather x1, waiting for transfers between devices, local(): lax.all_gather(cotangent, 'context', axis=0, tiled=True)  98.5 us
    psum x1, waiting for transfers between devices, local(): weight_sum = lax.psum(weight_acc.astype(jnp.bfloat16), 'dp')  51.4 us
    all_to_all x1, blocking collectives, local(): lax.all_to_all(activations, 'context', split_axis=1, concat_axis=0, tiled...  47.5 us
    dot_general x1, matrix products, accumulate(): lax.dot_general(heads_view, block_rows, (((0,), (0,)), ((), ())), preferr...  11.5 us
    dot_general x1, matrix products, accumulate(): lax.dot_general(block_rows, weight_cols, (((1,), (1,)), ((), ())), prefer...  9.93 us
  transfers between devices with their start and end apart: 2, of which 2 were waited for; matrix products, arithmetic and copies ran while one was open for 5% of the time, Pallas kernels for 0%

commit v1 on v0

v1 whole, which is shorter than its diff:
```python
import functools

import jax
import jax.numpy as jnp
from jax import lax
from jax.experimental import pallas as pl
from jax.experimental.pallas import tpu as pltpu
from jax.sharding import PartitionSpec as P

CHUNKS = 8
AHEAD = 2
CORES = 2


def grid_of(chips):
    fast = 1
    while (2 * fast) * (2 * fast) <= chips:
        fast *= 2
    return chips // fast, fast


def kernel(dp, n, chunks, g_in, a_in, w_in, o_attn, o_w, gath, acts, acts_t, w, acc, part, stage_w, stage_a,
           g_send, g_recv, a_send, a_recv, x_send, x_recv, own_sem, w_sem, own_a_sem, ow_sem, oa_sem):
    A, B = grid_of(n // CORES)
    tokens, width = g_in.shape
    heads = w_in.shape[0]
    F = width // chunks
    me = lax.axis_index("context")
    rep = lax.axis_index("dp")
    c = lax.rem(me, CORES)
    b = lax.rem(me // CORES, B)
    a = me // (CORES * B)

    def ctx(a_, b_, c_):
        return (a_ * B + b_) * CORES + c_

    def others(i, size):
        return [lax.rem(i + d, size) for d in range(1, size)]

    def cols(k):
        return pl.ds(pl.multiple_of(k * F, F), F)

    def rows(j):
        return pl.ds(pl.multiple_of(j * tokens, tokens), tokens)

    def block(k, j):
        return gath.at[k, rows(j)]

    def move(src, k, j, target, slot):
        return pltpu.make_async_remote_copy(
            src_ref=src, dst_ref=block(k, j), send_sem=g_send.at[k, slot], recv_sem=g_recv.at[k, j],
            device_id={"context": target}, device_id_type=pl.DeviceIdType.MESH)

    def arrived(k, j):
        move(block(k, j), k, j, me, 0).wait_recv()

    barrier = pltpu.get_barrier_semaphore()
    for j in others(me, n):
        pl.semaphore_signal(barrier, inc=1, device_id={"context": j}, device_id_type=pl.DeviceIdType.MESH)
    for r in others(rep, dp):
        pl.semaphore_signal(barrier, inc=1, device_id={"dp": r}, device_id_type=pl.DeviceIdType.MESH)
    pl.semaphore_wait(barrier, n - 1 + dp - 1)

    Z0, RELAY, Y0 = 0, A - 1, A
    S0 = Y0 + A * (B - 1)

    def own(k):
        return g_in.at[:, cols(k)]

    def skip_far(target):
        end = jnp.logical_or(target == 0, target == A - 1)
        return jnp.logical_and(end, jnp.logical_or(target == a + 2, target == a - 2))

    def z_moves(k, act):
        for i, t in enumerate(others(a, A)):
            @pl.when(jnp.logical_not(skip_far(t)))
            def _():
                act(move(own(k), k, me, ctx(t, b, c), Z0 + i))

    def y_own_moves(k, act):
        for i, t in enumerate(others(b, B)):
            act(move(own(k), k, me, ctx(a, t, c), Y0 + i))

    def sib_own(k, act):
        act(move(own(k), k, me, ctx(a, b, 1 - c), S0))

    def relay_moves(k, act):
        @pl.when(a == 1)
        def _():
            j = ctx(2, b, c)
            act(move(block(k, j), k, j, ctx(0, b, c), RELAY))
        if A != 3:
            @pl.when(a == A - 2)
            def _():
                j = ctx(A - 3, b, c)
                act(move(block(k, j), k, j, ctx(A - 1, b, c), RELAY))

    def column_moves(k, s, t, act):
        j = ctx(t, b, c)
        for i, u in enumerate(others(b, B)):
            act(move(block(k, j), k, j, ctx(a, u, c), Y0 + (s + 1) * (B - 1) + i))
        act(move(block(k, j), k, j, ctx(a, b, 1 - c), S0 + 1 + s))

    def plane_moves(k, act, wait):
        slot = S0 + A
        for u in others(b, B):
            for d in range(A):
                j = ctx(lax.rem(a + d, A), u, c)
                if wait:
                    arrived(k, j)
                act(move(block(k, j), k, j, ctx(a, b, 1 - c), slot))
                slot += 1

    def own_copy(k):
        return pltpu.make_async_copy(own(k), block(k, me), own_sem.at[k])

    def w_copy(k):
        return pltpu.make_async_copy(w_in.at[:, cols(k)], w.at[k], w_sem.at[k])

    def head_cols(j):
        return pl.ds(pl.multiple_of(j * heads, heads), heads)

    def act_move(i, target):
        return pltpu.make_async_remote_copy(
            src_ref=a_in.at[:, head_cols(target)], dst_ref=acts.at[me], send_sem=a_send.at[i],
            recv_sem=a_recv.at[me], device_id={"context": target}, device_id_type=pl.DeviceIdType.MESH)

    own_act = pltpu.make_async_copy(a_in.at[:, head_cols(me)], acts.at[me], own_a_sem)

    def start(m):
        m.start()

    def done(m):
        m.wait_send()

    def x_moves(k, act):
        for i, r in enumerate(others(rep, dp)):
            act(pltpu.make_async_remote_copy(
                src_ref=part.at[rep, k], dst_ref=part.at[rep, k], send_sem=x_send.at[k, i],
                recv_sem=x_recv.at[k, rep], device_id={"dp": r}, device_id_type=pl.DeviceIdType.MESH))

    def x_arrived(k):
        for r in others(rep, dp):
            pltpu.make_async_remote_copy(
                src_ref=part.at[r, k], dst_ref=part.at[r, k], send_sem=x_send.at[k, 0],
                recv_sem=x_recv.at[k, r], device_id={"dp": rep}, device_id_type=pl.DeviceIdType.MESH).wait_recv()

    z_moves(0, start)
    targets = others(me, n)
    for i, t in enumerate(targets):
        act_move(i, t).start()
    own_act.start()

    @pl.loop(0, chunks)
    def _(k):
        y_own_moves(k, start)
        sib_own(k, start)
        own_copy(k).start()
        w_copy(k).start()

    for k in range(1, AHEAD):
        z_moves(k, start)

    def columns(k):
        for s, t in enumerate(others(a, A)):
            arrived(k, ctx(t, b, c))
            column_moves(k, s, t, start)
        relay_moves(k, start)

    row_tile = min(512, tokens * n)
    tiles = tokens * n // row_tile

    def out_attn(i):
        r = pl.ds(pl.multiple_of(i * row_tile, row_tile), row_tile)
        return pltpu.make_async_copy(stage_a.at[r], o_attn.at[r], oa_sem.at[i])

    def compute(k):
        own_copy(k).wait()
        w_copy(k).wait()
        for t in range(A):
            for u in range(B):
                arrived(k, ctx(t, u, 1 - c))

        @pl.when(k == 0)
        def _():
            own_act.wait()
            for t in targets:
                pltpu.make_async_remote_copy(
                    src_ref=acts.at[t], dst_ref=acts.at[t], send_sem=a_send.at[0], recv_sem=a_recv.at[t],
                    device_id={"context": me}, device_id_type=pl.DeviceIdType.MESH).wait_recv()
            for j in range(n):
                acts_t[:, j * tokens:(j + 1) * tokens] = acts[j].T
            acc[...] = jnp.zeros_like(acc)

        part[rep, k] = jnp.dot(acts_t[...], gath[k], preferred_element_type=jnp.float32).astype(part.dtype)
        x_moves(k, start)

        @pl.loop(0, tiles)
        def _(i):
            r = pl.ds(pl.multiple_of(i * row_tile, row_tile), row_tile)
            total = acc[r] + lax.dot_general(
                gath[k, r], w[k], (((1,), (1,)), ((), ())), preferred_element_type=jnp.float32)

            @pl.when(k < chunks - 1)
            def _():
                acc[r] = total

            @pl.when(k == chunks - 1)
            def _():
                stage_a[r] = total.astype(stage_a.dtype)
                out_attn(i).start()

    def out_w(k):
        return pltpu.make_async_copy(stage_w.at[k], o_w.at[:, cols(k)], ow_sem.at[k])

    def finish(k):
        x_arrived(k)
        total = part[0, k].astype(jnp.float32)
        for r in range(1, dp):
            total += part[r, k].astype(jnp.float32)
        stage_w[k] = total.astype(stage_w.dtype)
        out_w(k).start()

    @pl.loop(0, chunks + 2)
    def _(i):
        @pl.when(i + AHEAD < chunks)
        def _():
            z_moves(i + AHEAD, start)

        @pl.when(i < chunks)
        def _():
            columns(i)

        @pl.when(jnp.logical_and(i >= 1, i <= chunks))
        def _():
            plane_moves(i - 1, start, True)
            compute(i - 1)

        @pl.when(i >= 2)
        def _():
            finish(i - 2)

    @pl.loop(0, chunks)
    def _(k):
        z_moves(k, done)
        y_own_moves(k, done)
        sib_own(k, done)
        for s, t in enumerate(others(a, A)):
            column_moves(k, s, t, done)
        relay_moves(k, done)
        plane_moves(k, done, False)
        x_moves(k, done)
        out_w(k).wait()

    for i, t in enumerate(targets):
        act_move(i, t).wait_send()

    @pl.loop(0, tiles)
    def _(i):
        out_attn(i).wait()


def local(dp, n, grad_out, attn, w_out):
    g, x = grad_out[0], attn[0]
    tokens, width = g.shape
    heads = w_out.shape[0]
    length = tokens * n
    chunks = CHUNKS
    F = width // chunks
    A, B = grid_of(n // CORES)
    sends = A + A * (B - 1) + A * B
    tiles = length // min(512, length)
    any_ = pl.BlockSpec(memory_space=pl.ANY)
    bf = jnp.bfloat16
    dma = pltpu.SemaphoreType.DMA
    h, gw = pl.pallas_call(
        functools.partial(kernel, dp, n, chunks),
        out_shape=(jax.ShapeDtypeStruct((length, heads), bf), jax.ShapeDtypeStruct((heads, width), bf)),
        in_specs=[any_] * 3,
        out_specs=(any_, any_),
        scratch_shapes=[
            pltpu.VMEM((chunks, length, F), bf),
            pltpu.VMEM((n, tokens, heads), bf),
            pltpu.VMEM((heads, length), bf),
            pltpu.VMEM((chunks, heads, F), bf),
            pltpu.VMEM((length, heads), jnp.float32),
            pltpu.VMEM((dp, chunks, heads, F), bf),
            pltpu.VMEM((chunks, heads, F), bf),
            pltpu.VMEM((length, heads), bf),
            dma((chunks, sends)), dma((chunks, n)), dma((n - 1,)), dma((n,)),
            dma((chunks, dp - 1)), dma((chunks, dp)),
            dma((chunks,)), dma((chunks,)), dma, dma((chunks,)), dma((tiles,)),
        ],
        compiler_params=pltpu.CompilerParams(
            collective_id=0, has_side_effects=True, vmem_limit_bytes=62 * 2**20),
    )(g, x, w_out)
    return h[None], gw


def solution(mesh):
    dp, n = mesh.shape["dp"], mesh.shape["context"]
    in_specs = (P("dp", "context", None), P("dp", "context", None), P("context", None))
    out_specs = (P("dp", None, "context"), P("context", None))
    return jax.shard_map(functools.partial(local, dp, n), mesh=mesh, in_specs=in_specs, out_specs=out_specs,
                         check_vma=False)
```

time: 240 us -> 141 us (0.59)
  waiting for transfers between devices: 151 us -> 0 us
  Pallas kernels: 0 us -> 137 us
  blocking collectives: 47.5 us -> 0 us
  matrix products: 21.4 us -> 0 us
  between operations: 14.1 us -> 0.65 us
  local copies, waits for them, and re-layouts: 6.24 us -> 3.73 us
    pallas_call x0 -> x1, Pallas kernels: none -> 137 us  [local(): pl.pallas_call(functools.partial(kernel, dp, n, chunks), out_shape=(jax.S...]
    all_gather x1 -> x0, waiting for transfers between devices: 98.5 us -> none  [local(): lax.all_gather(cotangent, 'context', axis=0, tiled=True)]
    psum x1 -> x0, waiting for transfers between devices: 51.4 us -> none  [local(): weight_sum = lax.psum(weight_acc.astype(jnp.bfloat16), 'dp')]
    all_to_all x1 -> x0, blocking collectives: 47.5 us -> none  [local(): lax.all_to_all(activations, 'context', split_axis=1, concat_axis=0, tiled...]
    dot_general x2 -> x0, matrix products: 21.4 us -> none  [the longest x1 11.5 us: accumulate(): lax.dot_general(heads_view, block_rows, (((0,), (0,)), ((), ())), preferr...]
  transfers between devices with their start and end apart: 2 -> 0, of which waited for: 2 -> 0; matrix products, arithmetic and copies ran while one was open for 5% -> 0% of each run, Pallas kernels for 0% -> 0%
where the time goes in v1:
time: 141 us
  Pallas kernels  137 us (97%)
  local copies, waits for them, and re-layouts  3.73 us (3%)
    pallas_call x1, Pallas kernels, local(): pl.pallas_call(functools.partial(kernel, dp, n, chunks), out_shape=(jax.S...  137 us
    unnamed x4, local copies, waits for them, and re-layouts  3.73 us

profile of v1, /device:TPU:0, one launch (start us, length us, event | category | flops | bytes accessed | tf_op | source)
XLA Modules:
  0.0 140.9 jit_solution(5737463570838344126)
XLA Ops:
  0.6 136.6 %shard_map.50 = (bf16[2048,256]{1,0:T(8,128)(2,1)}, bf16[256,4096]{1,0:T(8,128)(2,1)}) custom-call(bf16[128,4096]{1,0:T(8,128)(2,1)} %bitcast.4, bf16[128,4096]{1,0:T(8,128)(2,1)} %bitcast.5, bf16[256,4096]{1,0:T(8,128)(2,1)} %w_in.1), custom_call_target="tpu_custom_call" | custom-call | tf_op jit(solution)/shard_map/pallas_call | solution.py:276
  137.2 0.0 copy-start
  137.2 2.4 %copy.7 = bf16[1,2048,256]{2,1,0:T(8,128)(2,1)} copy(bf16[1,2048,256]{2,1,0:T(8,128)(2,1)} %bitcast.3) | data formatting | bytes 2097152
  139.6 0.0 copy-done
  139.6 1.3 copy.8
Async XLA Ops:
  137.2 2.4 %copy-start = (bf16[256,4096]{1,0:T(8,128)(2,1)S(1)}, bf16[256,4096]{1,0:T(8,128)(2,1)}, u32[]{:S(2)}) copy-start(bf16[256,4096]{1,0:T(8,128)(2,1)} %get-tuple-element.9) | copy-start | bytes 6291460

commit v2 on v1

--- a/solution.py
+++ b/solution.py
@@ -7,8 +7,9 @@
 from jax.experimental.pallas import tpu as pltpu
 from jax.sharding import PartitionSpec as P
 
-CHUNKS = 8
-AHEAD = 2
+CHUNKS = 16
+AHEAD = 3
+AHEAD_Y = 12
 CORES = 2
 
 
@@ -20,7 +21,7 @@
 
 
 def kernel(dp, n, chunks, g_in, a_in, w_in, o_attn, o_w, gath, acts, acts_t, w, acc, part, stage_w, stage_a,
-           g_send, g_recv, a_send, a_recv, x_send, x_recv, own_sem, w_sem, own_a_sem, ow_sem, oa_sem):
+           g_send, g_recv, p_send, p_recv, a_send, a_recv, x_send, x_recv, own_sem, w_sem, own_a_sem, ow_sem, oa_sem):
     A, B = grid_of(n // CORES)
     tokens, width = g_in.shape
     heads = w_in.shape[0]
@@ -61,55 +62,95 @@
         pl.semaphore_signal(barrier, inc=1, device_id={"dp": r}, device_id_type=pl.DeviceIdType.MESH)
     pl.semaphore_wait(barrier, n - 1 + dp - 1)
 
-    Z0, RELAY, Y0 = 0, A - 1, A
+    Z0, Y0 = 0, A + 1
     S0 = Y0 + A * (B - 1)
+    pair = a + 1 - 2 * lax.rem(a, 2)
+    side = 3 * tokens // 8
 
     def own(k):
         return g_in.at[:, cols(k)]
 
-    def skip_far(target):
-        end = jnp.logical_or(target == 0, target == A - 1)
-        return jnp.logical_and(end, jnp.logical_or(target == a + 2, target == a - 2))
+    def part_of(k, j, first):
+        size = side if first else tokens - side
+        lo = pl.multiple_of(j * tokens + (0 if first else side), 16)
+        return gath.at[k, pl.ds(lo, size)]
+
+    def inside(t):
+        return jnp.logical_and(t >= 0, t < A)
 
     def z_moves(k, act):
-        for i, t in enumerate(others(a, A)):
-            @pl.when(jnp.logical_not(skip_far(t)))
+        for sign, slot in ((1, Z0 + a), (-1, Z0 + A)):
+            @pl.when(inside(a + sign))
             def _():
-                act(move(own(k), k, me, ctx(t, b, c), Z0 + i))
+                act(move(own(k), k, me, ctx(a + sign, b, c), slot))
 
     def y_own_moves(k, act):
         for i, t in enumerate(others(b, B)):
-            act(move(own(k), k, me, ctx(a, t, c), Y0 + i))
+            act(move(own(k), k, me, ctx(a, t, c), Y0 + a * (B - 1) + i))
 
     def sib_own(k, act):
-        act(move(own(k), k, me, ctx(a, b, 1 - c), S0))
-
-    def relay_moves(k, act):
-        @pl.when(a == 1)
-        def _():
-            j = ctx(2, b, c)
-            act(move(block(k, j), k, j, ctx(0, b, c), RELAY))
-        if A != 3:
-            @pl.when(a == A - 2)
+        act(move(own(k), k, me, ctx(a, b, 1 - c), S0 + a))
+
+    def rest_move(k, j, target, slot):
+        return pltpu.make_async_remote_copy(
+            src_ref=part_of(k, j, False), dst_ref=part_of(k, j, False), send_sem=g_send.at[k, slot],
+            recv_sem=g_recv.at[k, j], device_id={"context": target}, device_id_type=pl.DeviceIdType.MESH)
+
+    def side_move(k, j, target, i):
+        return pltpu.make_async_remote_copy(
+            src_ref=part_of(k, j, True), dst_ref=part_of(k, j, True), send_sem=p_send.at[k, i],
+            recv_sem=p_recv.at[k, j], device_id={"context": target}, device_id_type=pl.DeviceIdType.MESH)
+
+    def side_moves(k, act, wait):
+        for i, u in enumerate(others(b, B)):
+            j = ctx(a, u, c)
+            if wait:
+                arrived(k, j)
+            act(side_move(k, j, ctx(pair, b, c), i))
+            act(move(block(k, j), k, j, ctx(a, b, 1 - c), S0 + A * (1 + i) + a))
+
+    def column_moves(k, d, act, wait):
+        for sign in (1, -1):
+            t = a + sign * d
+
+            @pl.when(inside(t))
             def _():
-                j = ctx(A - 3, b, c)
-                act(move(block(k, j), k, j, ctx(A - 1, b, c), RELAY))
-
-    def column_moves(k, s, t, act):
-        j = ctx(t, b, c)
-        for i, u in enumerate(others(b, B)):
-            act(move(block(k, j), k, j, ctx(a, u, c), Y0 + (s + 1) * (B - 1) + i))
-        act(move(block(k, j), k, j, ctx(a, b, 1 - c), S0 + 1 + s))
-
-    def plane_moves(k, act, wait):
-        slot = S0 + A
-        for u in others(b, B):
-            for d in range(A):
-                j = ctx(lax.rem(a + d, A), u, c)
+                j = ctx(t, b, c)
                 if wait:
                     arrived(k, j)
-                act(move(block(k, j), k, j, ctx(a, b, 1 - c), slot))
-                slot += 1
+
+                @pl.when(inside(a - sign))
+                def _():
+                    act(move(block(k, j), k, j, ctx(a - sign, b, c), Z0 + t))
+                for i, u in enumerate(others(b, B)):
+                    slot = Y0 + t * (B - 1) + i
+                    if d > 1:
+                        act(move(block(k, j), k, j, ctx(a, u, c), slot))
+                    else:
+                        @pl.when(t == pair)
+                        def _():
+                            act(rest_move(k, j, ctx(a, u, c), slot))
+
+                        @pl.when(t != pair)
+                        def _():
+                            act(move(block(k, j), k, j, ctx(a, u, c), slot))
+                act(move(block(k, j), k, j, ctx(a, b, 1 - c), S0 + t))
+
+    def plane_moves(k, act, wait):
+        for i, u in enumerate(others(b, B)):
+            for d in range(1, A):
+                t = lax.rem(a + d, A)
+                j = ctx(t, u, c)
+                if wait:
+                    @pl.when(t == pair)
+                    def _():
+                        rest_move(k, j, me, 0).wait_recv()
+                        side_move(k, j, me, 0).wait_recv()
+
+                    @pl.when(t != pair)
+                    def _():
+                        arrived(k, j)
+                act(move(block(k, j), k, j, ctx(a, b, 1 - c), S0 + A * (1 + i) + t))
 
     def own_copy(k):
         return pltpu.make_async_copy(own(k), block(k, me), own_sem.at[k])
@@ -145,27 +186,21 @@
                 src_ref=part.at[r, k], dst_ref=part.at[r, k], send_sem=x_send.at[k, 0],
                 recv_sem=x_recv.at[k, r], device_id={"dp": rep}, device_id_type=pl.DeviceIdType.MESH).wait_recv()
 
-    z_moves(0, start)
+    for k in range(AHEAD):
+        z_moves(k, start)
     targets = others(me, n)
     for i, t in enumerate(targets):
         act_move(i, t).start()
     own_act.start()
 
+    for k in range(AHEAD_Y):
+        y_own_moves(k, start)
+        sib_own(k, start)
+
     @pl.loop(0, chunks)
     def _(k):
-        y_own_moves(k, start)
-        sib_own(k, start)
         own_copy(k).start()
         w_copy(k).start()
-
-    for k in range(1, AHEAD):
-        z_moves(k, start)
-
-    def columns(k):
-        for s, t in enumerate(others(a, A)):
-            arrived(k, ctx(t, b, c))
-            column_moves(k, s, t, start)
-        relay_moves(k, start)
 
     row_tile = min(512, tokens * n)
     tiles = tokens * n // row_tile
@@ -221,33 +256,36 @@
         stage_w[k] = total.astype(stage_w.dtype)
         out_w(k).start()
 
-    @pl.loop(0, chunks + 2)
+    def stage(k, f):
+        pl.when(jnp.logical_and(k >= 0, k < chunks))(functools.partial(f, k))
+
+    @pl.loop(0, chunks + A + 2)
     def _(i):
-        @pl.when(i + AHEAD < chunks)
-        def _():
-            z_moves(i + AHEAD, start)
-
-        @pl.when(i < chunks)
-        def _():
-            columns(i)
-
-        @pl.when(jnp.logical_and(i >= 1, i <= chunks))
-        def _():
-            plane_moves(i - 1, start, True)
-            compute(i - 1)
-
-        @pl.when(i >= 2)
-        def _():
-            finish(i - 2)
+        def ahead_z(k):
+            z_moves(k, start)
+
+        def ahead_y(k):
+            y_own_moves(k, start)
+            sib_own(k, start)
+
+        stage(i + AHEAD, ahead_z)
+        stage(i + AHEAD_Y, ahead_y)
+        for d in range(1, A):
+            stage(i - d + 1, lambda k, d=d: column_moves(k, d, start, True))
+            if d == 1:
+                stage(i, lambda k: side_moves(k, start, True))
+        stage(i - A + 1, lambda k: plane_moves(k, start, True))
+        stage(i - A, compute)
+        stage(i - A - 1, finish)
 
     @pl.loop(0, chunks)
     def _(k):
         z_moves(k, done)
         y_own_moves(k, done)
         sib_own(k, done)
-        for s, t in enumerate(others(a, A)):
-            column_moves(k, s, t, done)
-        relay_moves(k, done)
+        side_moves(k, done, False)
+        for d in range(1, A):
+            column_moves(k, d, done, False)
         plane_moves(k, done, False)
         x_moves(k, done)
         out_w(k).wait()
@@ -268,7 +306,7 @@
     chunks = CHUNKS
     F = width // chunks
     A, B = grid_of(n // CORES)
-    sends = A + A * (B - 1) + A * B
+    sends = A + 1 + A * (B - 1) + A * B
     tiles = length // min(512, length)
     any_ = pl.BlockSpec(memory_space=pl.ANY)
     bf = jnp.bfloat16
@@ -287,7 +325,8 @@
             pltpu.VMEM((dp, chunks, heads, F), bf),
             pltpu.VMEM((chunks, heads, F), bf),
             pltpu.VMEM((length, heads), bf),
-            dma((chunks, sends)), dma((chunks, n)), dma((n - 1,)), dma((n,)),
+            dma((chunks, sends)), dma((chunks, n)), dma((chunks, B - 1)), dma((chunks, n)),
+            dma((n - 1,)), dma((n,)),
             dma((chunks, dp - 1)), dma((chunks, dp)),
             dma((chunks,)), dma((chunks,)), dma, dma((chunks,)), dma((tiles,)),
         ],

time: 141 us -> 132 us (0.936)
  Pallas kernels: 137 us -> 127 us
    pallas_call x1, Pallas kernels: 137 us -> 127 us  [local(): pl.pallas_call(functools.partial(kernel, dp, n, chunks), out_shape=(jax.S...]
where the time goes in v2:
time: 132 us
  Pallas kernels  127 us (96%)
  local copies, waits for them, and re-layouts  3.73 us (3%)
    pallas_call x1, Pallas kernels, local(): pl.pallas_call(functools.partial(kernel, dp, n, chunks), out_shape=(jax.S...  127 us
    unnamed x4, local copies, waits for them, and re-layouts  3.73 us

profile of v2, /device:TPU:0, one launch (start us, length us, event | category | flops | bytes accessed | tf_op | source)
XLA Modules:
  0.0 131.6 jit_solution(1022470100341000622)
XLA Ops:
  0.6 127.2 %shard_map.50 = (bf16[2048,256]{1,0:T(8,128)(2,1)}, bf16[256,4096]{1,0:T(8,128)(2,1)}) custom-call(bf16[128,4096]{1,0:T(8,128)(2,1)} %bitcast.4, bf16[128,4096]{1,0:T(8,128)(2,1)} %bitcast.5, bf16[256,4096]{1,0:T(8,128)(2,1)} %w_in.1), custom_call_target="tpu_custom_call" | custom-call | tf_op jit(solution)/shard_map/pallas_call | solution.py:314
  127.9 0.0 copy-start
  127.9 2.4 %copy.7 = bf16[1,2048,256]{2,1,0:T(8,128)(2,1)} copy(bf16[1,2048,256]{2,1,0:T(8,128)(2,1)} %bitcast.3) | data formatting | bytes 2097152
  130.3 0.0 copy-done
  130.3 1.3 %copy.8 = bf16[256,4096]{1,0:T(8,128)(2,1)} copy(bf16[256,4096]{1,0:T(8,128)(2,1)S(1)} %copy-done) | data formatting | bytes 4194304
Async XLA Ops:
  127.9 2.4 %copy-start = (bf16[256,4096]{1,0:T(8,128)(2,1)S(1)}, bf16[256,4096]{1,0:T(8,128)(2,1)}, u32[]{:S(2)}) copy-start(bf16[256,4096]{1,0:T(8,128)(2,1)} %get-tuple-element.9) | copy-start | bytes 6291460

commit v3 on v2

--- a/solution.py
+++ b/solution.py
@@ -8,8 +8,8 @@
 from jax.sharding import PartitionSpec as P
 
 CHUNKS = 16
-AHEAD = 3
-AHEAD_Y = 12
+AHEAD = 2
+AHEAD_Y = 8
 CORES = 2
 
 
@@ -65,7 +65,7 @@
     Z0, Y0 = 0, A + 1
     S0 = Y0 + A * (B - 1)
     pair = a + 1 - 2 * lax.rem(a, 2)
-    side = 3 * tokens // 8
+    side = tokens // 4
 
     def own(k):
         return g_in.at[:, cols(k)]
@@ -331,7 +331,7 @@
             dma((chunks,)), dma((chunks,)), dma, dma((chunks,)), dma((tiles,)),
         ],
         compiler_params=pltpu.CompilerParams(
-            collective_id=0, has_side_effects=True, vmem_limit_bytes=62 * 2**20),
+            collective_id=0, has_side_effects=True, vmem_limit_bytes=52 * 2**20),
     )(g, x, w_out)
     return h[None], gw
 

time: 132 us -> 129 us (0.977)
  Pallas kernels: 127 us -> 125 us
    pallas_call x1, Pallas kernels: 127 us -> 125 us  [local(): pl.pallas_call(functools.partial(kernel, dp, n, chunks), out_shape=(jax.S...]
where the time goes in v3:
time: 129 us
  Pallas kernels  125 us (97%)
  local copies, waits for them, and re-layouts  3.28 us (3%)
    pallas_call x1, Pallas kernels, local(): pl.pallas_call(functools.partial(kernel, dp, n, chunks), out_shape=(jax.S...  125 us
    unnamed x4, local copies, waits for them, and re-layouts  3.28 us

profile of v3, /device:TPU:0, one launch (start us, length us, event | category | flops | bytes accessed | tf_op | source)
XLA Modules:
  0.0 128.8 jit_solution(7515429874484122125)
XLA Ops:
  0.6 124.9 %shard_map.50 = (bf16[2048,256]{1,0:T(8,128)(2,1)S(1)}, bf16[256,4096]{1,0:T(8,128)(2,1)}) custom-call(bf16[128,4096]{1,0:T(8,128)(2,1)} %bitcast.4, bf16[128,4096]{1,0:T(8,128)(2,1)} %bitcast.5, bf16[256,4096]{1,0:T(8,128)(2,1)} %w_in.1), custom_call_target="tpu_custom_call" | custom-call | tf_op jit(solution)/shard_map/pallas_call | solution.py:314
  125.5 0.0 copy-start
  125.5 1.0 copy.7
  126.5 1.0 copy-done
  127.5 1.3 %copy.8 = bf16[256,4096]{1,0:T(8,128)(2,1)} copy(bf16[256,4096]{1,0:T(8,128)(2,1)S(1)} %copy-done) | data formatting | bytes 4194304
Async XLA Ops:
  125.5 2.0 %copy-start = (bf16[256,4096]{1,0:T(8,128)(2,1)S(1)}, bf16[256,4096]{1,0:T(8,128)(2,1)}, u32[]{:S(2)}) copy-start(bf16[256,4096]{1,0:T(8,128)(2,1)} %get-tuple-element.9) | copy-start | bytes 6291460
